TPU v7x, 32 devices: a whole 2x2x4 slice. The times are simulated.
32 devices in a mesh: dp: 2 (over x), context: 4 (over y, core), tensor: 4 (over z).
Axes of the slice: x: 2, y: 2, z: 4, core: 2. Of those that a mesh axis runs over, the one named last changes fastest.
Arguments:
- hidden_in: bfloat16 [16, 1024, 576], P('dp', ('context', 'tensor')), may hold values from -6 to 6
- attn_gain: bfloat16 [576], P('dp'), may hold values from 0.099609375 to 1.8984375
- query_weight: bfloat16 [576, 576], P('dp'), may hold values from -0.25 to 0.25
- key_weight: bfloat16 [576, 192], P('dp'), may hold values from -0.25 to 0.25
- value_weight: bfloat16 [576, 192], P('dp'), may hold values from -0.25 to 0.25
- output_weight: bfloat16 [576, 576], P('dp'), may hold values from -3 to 3
- ffn_gain: bfloat16 [576], P('dp'), may hold values from 0.099609375 to 1.8984375
- gate_weight: bfloat16 [576, 1536], P('dp', 'tensor'), may hold values from -0.25 to 0.25
- up_weight: bfloat16 [576, 1536], P('dp', 'tensor'), may hold values from -0.25 to 0.25
- down_weight: bfloat16 [1536, 576], P('tensor', 'dp'), may hold values from -0.15625 to 0.15625
- out_grad: bfloat16 [16, 1024, 576], P('dp', ('context', 'tensor')), may hold values from -6 to 6
Outputs:
- hidden_out: bfloat16 [16, 1024, 576], P('dp', ('context', 'tensor'))
- input_grad: float32 [16, 1024, 576], P('dp', ('context', 'tensor'))
- attn_gain_grad: float32 [576], P('dp')
- query_weight_grad: float32 [576, 576], P('dp')
- key_weight_grad: float32 [576, 192], P('dp')
- value_weight_grad: float32 [576, 192], P('dp')
- output_weight_grad: float32 [576, 576], P('dp')
- ffn_gain_grad: float32 [576], P('dp')
- gate_weight_grad: float32 [576, 1536], P('dp', 'tensor')
- up_weight_grad: float32 [576, 1536], P('dp', 'tensor')
- down_weight_grad: float32 [1536, 576], P('tensor', 'dp')
All inputs are finite; a program needn't handle non-finite values.
Results may differ from a plain program's by a relative error of at most 0.024.
Values may be sent and summed in bfloat16 or wider, within the bound.
No kernel may reach another device: no remote copies, remote signals or barrier semaphores. Data moves between devices by JAX's collectives and lax.ppermute only.
A program may use at most 128 MiB of HBM per device.

v0:
```python
import jax
import jax.numpy as jnp
from jax import lax
from jax.sharding import PartitionSpec as P

HEADS = 9
KV_HEADS = 3
HEAD_DIM = 64
EPS = 1e-05
ROPE_BASE = 100000.0


def rotary(places, half_dim):
    frequency = ROPE_BASE ** (-jnp.arange(half_dim).astype(jnp.float32) / half_dim)
    angles = places.astype(jnp.float32)[:, None] * frequency[None, :]
    return (jnp.cos(angles), jnp.sin(angles))


def rotate(tensor, cosine_table, sine_table):
    half_dim = tensor.shape[-1] // 2
    first_half = tensor[..., :half_dim]
    second_half = tensor[..., half_dim:]
    cosine_b = cosine_table[:, None, :]
    sine_b = sine_table[:, None, :]
    return jnp.concatenate(
        [
            first_half * cosine_b - second_half * sine_b,
            second_half * cosine_b + first_half * sine_b,
        ],
        axis=-1,
    )


def rotate_back(tensor, cosine_table, sine_table):
    half_dim = tensor.shape[-1] // 2
    first_half = tensor[..., :half_dim]
    second_half = tensor[..., half_dim:]
    cosine_b = cosine_table[:, None, :]
    sine_b = sine_table[:, None, :]
    return jnp.concatenate(
        [
            first_half * cosine_b + second_half * sine_b,
            second_half * cosine_b - first_half * sine_b,
        ],
        axis=-1,
    )


def times_transposed(left, right):
    return lax.dot_general(
        left, right, (((1,), (1,)), ((), ())), preferred_element_type=jnp.float32
    )


def transposed_times(left, right):
    return lax.dot_general(
        left, right, (((0,), (0,)), ((), ())), preferred_element_type=jnp.float32
    )


def norm_back(grad_normed, normed, inverse):
    return inverse * (grad_normed - normed * jnp.mean(grad_normed * normed, axis=-1, keepdims=True))


def body(
    hidden_in,
    attn_gain,
    query_weight,
    key_weight,
    value_weight,
    output_weight,
    ffn_gain,
    gate_weight,
    up_weight,
    down_weight,
    out_grad,
):
    seq_count, local_len, model_width = hidden_in.shape
    kv_width = KV_HEADS * HEAD_DIM
    repeat = HEADS // KV_HEADS
    scale = HEAD_DIM ** (-0.5)
    token_rows = seq_count * local_len
    gain_one, query_all, key_all, value_all, output_all = (
        lax.all_gather(attn_gain, "dp", axis=0, tiled=True),
        lax.all_gather(query_weight, "dp", axis=0, tiled=True),
        lax.all_gather(key_weight, "dp", axis=0, tiled=True),
        lax.all_gather(value_weight, "dp", axis=0, tiled=True),
        lax.all_gather(output_weight, "dp", axis=0, tiled=True),
    )
    gain_two, gate_all, up_all, down_all = (
        lax.all_gather(ffn_gain, "dp", axis=0, tiled=True),
        lax.all_gather(gate_weight, "dp", axis=0, tiled=True),
        lax.all_gather(up_weight, "dp", axis=0, tiled=True),
        lax.all_gather(down_weight, "dp", axis=1, tiled=True),
    )
    places = lax.axis_index(("context", "tensor")) * local_len + jnp.arange(
        local_len, dtype=jnp.int32
    )
    cosine_table, sine_table = rotary(places, HEAD_DIM // 2)
    rows_in = hidden_in.astype(jnp.float32)
    inverse_one = lax.rsqrt(jnp.mean(rows_in * rows_in, axis=-1, keepdims=True) + EPS)
    normed_one = rows_in * inverse_one
    normed_low = (normed_one * gain_one.astype(jnp.float32)).astype(jnp.bfloat16)
    flat_normed = normed_low.reshape(token_rows, model_width)
    queries = jnp.dot(flat_normed, query_all, preferred_element_type=jnp.float32).reshape(
        seq_count, local_len, HEADS, HEAD_DIM
    )
    key_rows = jnp.dot(flat_normed, key_all, preferred_element_type=jnp.float32).reshape(
        seq_count, local_len, KV_HEADS, HEAD_DIM
    )
    value_rows = jnp.dot(flat_normed, value_all, preferred_element_type=jnp.float32).reshape(
        seq_count, local_len, kv_width
    )
    queries_low = rotate(queries, cosine_table, sine_table).astype(jnp.bfloat16)
    keys_low = (
        rotate(key_rows, cosine_table, sine_table)
        .astype(jnp.bfloat16)
        .reshape(seq_count, local_len, kv_width)
    )
    kv_local = jnp.concatenate([keys_low, value_rows.astype(jnp.bfloat16)], axis=-1)
    kv_whole = lax.all_gather(kv_local, ("context", "tensor"), axis=1, tiled=True)
    seq_len = kv_whole.shape[1]
    query_groups = queries_low.reshape(seq_count, local_len, KV_HEADS, repeat, HEAD_DIM)

    def attend_one(operands):
        query_seq, kv_seq = operands
        key_seq = kv_seq[:, :kv_width].reshape(seq_len, KV_HEADS, HEAD_DIM)
        value_seq = kv_seq[:, kv_width:].reshape(seq_len, KV_HEADS, HEAD_DIM)
        scores = (
            jnp.einsum("qgre,kge->grqk", query_seq, key_seq, preferred_element_type=jnp.float32)
            * scale
        )
        allowed = jnp.arange(seq_len)[None, :] <= places[:, None]
        scores = jnp.where(allowed, scores, -1e30)
        row_max = jnp.max(scores, axis=-1, keepdims=True)
        weights = jnp.exp(scores - row_max)
        row_sum = jnp.sum(weights, axis=-1, keepdims=True)
        probability = (weights / row_sum).astype(jnp.bfloat16)
        attended_seq = jnp.einsum(
            "grqk,kge->qgre", probability, value_seq, preferred_element_type=jnp.float32
        )
        return (
            attended_seq.reshape(local_len, HEADS * HEAD_DIM),
            row_max[..., 0] + jnp.log(row_sum[..., 0]),
        )

    attended, log_sums = lax.map(attend_one, (query_groups, kv_whole))
    attended_low = attended.astype(jnp.bfloat16)
    attended_flat = attended_low.reshape(token_rows, HEADS * HEAD_DIM)
    middle = rows_in + jnp.dot(
        attended_flat, output_all, preferred_element_type=jnp.float32
    ).reshape(seq_count, local_len, model_width)
    inverse_two = lax.rsqrt(jnp.mean(middle * middle, axis=-1, keepdims=True) + EPS)
    normed_two = middle * inverse_two
    ffn_low = (normed_two * gain_two.astype(jnp.float32)).astype(jnp.bfloat16)
    ffn_rows = lax.all_gather(ffn_low, "tensor", axis=1, tiled=True)
    block_len = ffn_rows.shape[1]
    wide_rows = seq_count * block_len
    flat_rows = ffn_rows.reshape(wide_rows, model_width)
    gate_act = jnp.dot(flat_rows, gate_all, preferred_element_type=jnp.float32)
    up_act = jnp.dot(flat_rows, up_all, preferred_element_type=jnp.float32)
    sigmoid_gate = jax.nn.sigmoid(gate_act)
    silu_act = gate_act * sigmoid_gate
    hidden_low = (silu_act * up_act).astype(jnp.bfloat16)
    partial_out = jnp.dot(hidden_low, down_all, preferred_element_type=jnp.float32).reshape(
        seq_count, block_len, model_width
    )
    ffn_out = lax.psum_scatter(
        partial_out.astype(jnp.bfloat16), "tensor", scatter_dimension=1, tiled=True
    ).astype(jnp.float32)
    hidden_out = (middle + ffn_out).astype(jnp.bfloat16)
    grad_rows = lax.all_gather(out_grad, "tensor", axis=1, tiled=True).reshape(
        wide_rows, model_width
    )
    grad_hidden = times_transposed(grad_rows, down_all)
    down_grad = transposed_times(hidden_low, grad_rows)
    grad_up_low = (grad_hidden * silu_act).astype(jnp.bfloat16)
    grad_gate_low = (
        grad_hidden * up_act * (sigmoid_gate * (1.0 + gate_act * (1.0 - sigmoid_gate)))
    ).astype(jnp.bfloat16)
    gate_grad = transposed_times(flat_rows, grad_gate_low)
    up_grad = transposed_times(flat_rows, grad_up_low)
    grad_ffn_part = (
        times_transposed(grad_gate_low, gate_all) + times_transposed(grad_up_low, up_all)
    ).reshape(seq_count, block_len, model_width)
    grad_ffn_in = lax.psum_scatter(
        grad_ffn_part.astype(jnp.bfloat16), "tensor", scatter_dimension=1, tiled=True
    ).astype(jnp.float32)
    ffn_gain_term = jnp.sum(grad_ffn_in * normed_two, axis=(0, 1))
    grad_middle = out_grad.astype(jnp.float32) + norm_back(
        grad_ffn_in * gain_two.astype(jnp.float32), normed_two, inverse_two
    )
    grad_mid_low = grad_middle.astype(jnp.bfloat16).reshape(token_rows, model_width)
    out_proj_grad = transposed_times(attended_flat, grad_mid_low)
    grad_attended = (
        times_transposed(grad_mid_low, output_all)
        .astype(jnp.bfloat16)
        .reshape(seq_count, local_len, KV_HEADS, repeat, HEAD_DIM)
    )
    attended_groups = attended.reshape(seq_count, local_len, KV_HEADS, repeat, HEAD_DIM)
    row_delta = jnp.transpose(
        jnp.sum(grad_attended.astype(jnp.float32) * attended_groups, axis=-1), (0, 2, 3, 1)
    )
    piece = lax.all_gather(kv_local, ("context", "tensor"), axis=1, tiled=True)
    piece_len = piece.shape[1]
    key_piece = piece[..., :kv_width].reshape(seq_count, piece_len, KV_HEADS, HEAD_DIM)
    value_piece = piece[..., kv_width:].reshape(seq_count, piece_len, KV_HEADS, HEAD_DIM)
    scores = (
        jnp.einsum("sqgre,skge->sgrqk", query_groups, key_piece, preferred_element_type=jnp.float32)
        * scale
    )
    allowed = jnp.arange(piece_len)[None, :] <= places[:, None]
    probs_full = jnp.exp(jnp.where(allowed, scores - log_sums[..., None], -1e30))
    grad_probs = jnp.einsum(
        "sqgre,skge->sgrqk", grad_attended, value_piece, preferred_element_type=jnp.float32
    )
    grad_scores = (probs_full * (grad_probs - row_delta[..., None])).astype(jnp.bfloat16)
    key_piece, probs_full, grad_scores = (key_piece, probs_full, grad_scores)
    grad_query = (
        jnp.einsum("sgrqk,skge->sqgre", grad_scores, key_piece, preferred_element_type=jnp.float32)
        * scale
    )
    piece_len = piece.shape[1]
    grad_keys = (
        jnp.einsum(
            "sgrqk,sqgre->skge", grad_scores, query_groups, preferred_element_type=jnp.float32
        )
        * scale
    )
    grad_values = jnp.einsum(
        "sgrqk,sqgre->skge",
        probs_full.astype(jnp.bfloat16),
        grad_attended,
        preferred_element_type=jnp.float32,
    )
    grad_piece = jnp.concatenate(
        [
            grad_keys.reshape(seq_count, piece_len, kv_width),
            grad_values.reshape(seq_count, piece_len, kv_width),
        ],
        axis=-1,
    )
    grad_kv = grad_piece
    grad_query, grad_kv = (grad_query, grad_kv)
    grad_kv_own = lax.psum_scatter(
        grad_kv.astype(jnp.bfloat16), ("context", "tensor"), scatter_dimension=1, tiled=True
    ).astype(jnp.float32)
    grad_keys_low = (
        rotate_back(
            grad_kv_own[..., :kv_width].reshape(seq_count, local_len, KV_HEADS, HEAD_DIM),
            cosine_table,
            sine_table,
        )
        .astype(jnp.bfloat16)
        .reshape(token_rows, kv_width)
    )
    grad_values_low = grad_kv_own[..., kv_width:].astype(jnp.bfloat16).reshape(token_rows, kv_width)
    grad_query_low = (
        rotate_back(
            grad_query.reshape(seq_count, local_len, HEADS, HEAD_DIM), cosine_table, sine_table
        )
        .astype(jnp.bfloat16)
        .reshape(token_rows, HEADS * HEAD_DIM)
    )
    query_grad = transposed_times(flat_normed, grad_query_low)
    key_grad = transposed_times(flat_normed, grad_keys_low)
    value_grad = transposed_times(flat_normed, grad_values_low)
    grad_normed = (
        times_transposed(grad_query_low, query_all)
        + times_transposed(grad_keys_low, key_all)
        + times_transposed(grad_values_low, value_all)
    )
    grad_normed = grad_normed.reshape(seq_count, local_len, model_width)
    attn_gain_term = jnp.sum(grad_normed * normed_one, axis=(0, 1))
    input_grad = grad_middle + norm_back(
        grad_normed * gain_one.astype(jnp.float32), normed_one, inverse_one
    )
    shards = (
        lax.psum_scatter(
            attn_gain_term.astype(jnp.bfloat16), "dp", scatter_dimension=0, tiled=True
        ).astype(jnp.float32),
        lax.psum_scatter(
            ffn_gain_term.astype(jnp.bfloat16), "dp", scatter_dimension=0, tiled=True
        ).astype(jnp.float32),
        lax.psum_scatter(
            query_grad.astype(jnp.bfloat16), "dp", scatter_dimension=0, tiled=True
        ).astype(jnp.float32),
        lax.psum_scatter(
            key_grad.astype(jnp.bfloat16), "dp", scatter_dimension=0, tiled=True
        ).astype(jnp.float32),
        lax.psum_scatter(
            value_grad.astype(jnp.bfloat16), "dp", scatter_dimension=0, tiled=True
        ).astype(jnp.float32),
        lax.psum_scatter(
            out_proj_grad.astype(jnp.bfloat16), "dp", scatter_dimension=0, tiled=True
        ).astype(jnp.float32),
        lax.psum_scatter(
            gate_grad.astype(jnp.bfloat16), "dp", scatter_dimension=0, tiled=True
        ).astype(jnp.float32),
        lax.psum_scatter(
            up_grad.astype(jnp.bfloat16), "dp", scatter_dimension=0, tiled=True
        ).astype(jnp.float32),
        lax.psum_scatter(
            down_grad.astype(jnp.bfloat16), "dp", scatter_dimension=1, tiled=True
        ).astype(jnp.float32),
    )
    attn_sums = (
        lax.psum(shards[0].astype(jnp.bfloat16), ("context", "tensor")).astype(jnp.float32),
        lax.psum(shards[1].astype(jnp.bfloat16), ("context", "tensor")).astype(jnp.float32),
        lax.psum(shards[2].astype(jnp.bfloat16), ("context", "tensor")).astype(jnp.float32),
        lax.psum(shards[3].astype(jnp.bfloat16), ("context", "tensor")).astype(jnp.float32),
        lax.psum(shards[4].astype(jnp.bfloat16), ("context", "tensor")).astype(jnp.float32),
        lax.psum(shards[5].astype(jnp.bfloat16), ("context", "tensor")).astype(jnp.float32),
    )
    ffn_sums = (
        lax.psum(shards[6].astype(jnp.bfloat16), "context").astype(jnp.float32),
        lax.psum(shards[7].astype(jnp.bfloat16), "context").astype(jnp.float32),
        lax.psum(shards[8].astype(jnp.bfloat16), "context").astype(jnp.float32),
    )
    return (
        hidden_out,
        input_grad,
        attn_sums[0],
        attn_sums[2],
        attn_sums[3],
        attn_sums[4],
        attn_sums[5],
        attn_sums[1],
        ffn_sums[0],
        ffn_sums[1],
        ffn_sums[2],
    )


def solution(mesh):
    placed = (
        P("dp", ("context", "tensor"), None),
        P("dp"),
        P("dp", None),
        P("dp", None),
        P("dp", None),
        P("dp", None),
        P("dp"),
        P("dp", "tensor"),
        P("dp", "tensor"),
        P("tensor", "dp"),
        P("dp", ("context", "tensor"), None),
    )
    return jax.shard_map(
        body,
        mesh=mesh,
        in_specs=placed,
        out_specs=(
            P("dp", ("context", "tensor"), None),
            P("dp", ("context", "tensor"), None),
            P("dp"),
            P("dp", None),
            P("dp", None),
            P("dp", None),
            P("dp", None),
            P("dp"),
            P("dp", "tensor"),
            P("dp", "tensor"),
            P("tensor", "dp"),
        ),
        check_vma=False,
    )
```

profile of v0, /device:TPU:0, one launch (start us, length us, event | category | flops | bytes accessed | tf_op | source)
XLA Modules:
  0.0 730.7 jit_solution(6010033176116477348)
XLA Ops:
  11.0 5.8 all-reduce.8
  18.2 6.1 all_gather.38
  25.0 6.0 all_gather.39
  33.8 8.2 %all_gather.41 = bf16[576,576]{1,0:T(8,128)(2,1)S(1)} all-gather(bf16[288,576]{1,0:T(8,128)(2,1)S(1)} %copy-done.29), channel_id=1, replica_groups=mesh['dp'=2,'context'=4,'tensor'=4] {'dp'}, dimensions={0}, use_global_device_ids=true | all-gather | bytes 995328 | tf_op jit(solution)/shard_map/all_gather | solution.py:85
  47.8 8.3 %all_gather.42 = bf16[576,576]{1,0:T(8,128)(2,1)} all-gather(bf16[288,576]{1,0:T(8,128)(2,1)S(1)} %copy-done.30), channel_id=1, replica_groups=mesh['dp'=2,'context'=4,'tensor'=4] {'dp'}, dimensions={0}, use_global_device_ids=true | all-gather | bytes 995328 | tf_op jit(solution)/shard_map/all_gather | solution.py:88
  56.1 40.9 %all-gather.4.cloned.1.call-done = bf16[8,1024,384]{2,1,0:T(8,128)(2,1)} async-done(((bf16[8,64,384]{2,1,0:T(8,128)(2,1)}), bf16[8,1024,384]{2,1,0:T(8,128)(2,1)}) %all-gather.4.cloned.1.call-update) | async-done | bytes 6291472 | tf_op jit(solution)/shard_map/all_gather | solution.py:121
  97.0 41.1 %while.13 = (s32[]{:T(128)}, f32[8,64,576]{1,2,0:T(8,128)}, f32[8,3,3,64]{3,2,1,0:T(4,128)}, bf16[8,1024,384]{2,1,0:T(8,128)(2,1)}, bf16[8,64,3,3,64]{4,1,3,2,0:T(8,128)(2,1)S(1)}, /*index=5*/s32[]{:T(128)}, s32[]{:T(128)}) while((s32[]{:T(128)}, f32[8,64,576]{1,2,0:T(8,128)}, f32[8,3,3,64]{3,2,1,0:T(4,128)}, ...), condition=%wide.region_4.5_spmd.clone, body=%wide.region_1.4_spmd.clone.sunk | while | flops 158137856 | bytes 13605225 | solution.py:147
  138.1 3.2 multiply_reduce_fusion
  144.2 8.4 %all_gather.45 = bf16[576,384]{1,0:T(8,128)(2,1)} all-gather(bf16[288,384]{1,0:T(8,128)(2,1)S(1)} %copy-done.31), channel_id=1, replica_groups=mesh['dp'=2,'context'=4,'tensor'=4] {'dp'}, dimensions={0}, use_global_device_ids=true | all-gather | bytes 663552 | tf_op jit(solution)/shard_map/all_gather | solution.py:92
  152.6 7.5 %all_gather.46 = bf16[576,384]{1,0:T(8,128)(2,1)} all-gather(bf16[288,384]{1,0:T(8,128)(2,1)S(1)} %copy-done.32), channel_id=1, replica_groups=mesh['dp'=2,'context'=4,'tensor'=4] {'dp'}, dimensions={0}, use_global_device_ids=true | all-gather | bytes 663552 | tf_op jit(solution)/shard_map/all_gather | solution.py:93
  160.1 6.9 all_gather.47
  166.9 30.1 %all-gather.6.cloned.1.call-done = bf16[8,256,576]{2,1,0:T(8,128)(2,1)} async-done(((bf16[8,64,576]{2,1,0:T(8,128)(2,1)}), bf16[8,256,576]{2,1,0:T(8,128)(2,1)}) %all-gather.6.cloned.1.call-update) | async-done | bytes 2359312 | tf_op jit(solution)/shard_map/all_gather | solution.py:156
  197.0 3.6 fusion.65
  200.7 3.4 fusion.64
  204.1 48.1 %all-gather.8.cloned.1.call-done = bf16[8,256,576]{2,1,0:T(8,128)(2,1)} async-done(((bf16[8,64,576]{2,1,0:T(8,128)(2,1)}), bf16[8,256,576]{2,1,0:T(8,128)(2,1)}) %all-gather.8.cloned.1.call-update) | async-done | bytes 2359312 | tf_op jit(solution)/shard_map/all_gather | solution.py:172
  252.2 6.8 multiply_convert_fusion
  262.0 2.6 copy.73
  266.3 3.6 convolution_convert_fusion.3
  270.2 6.6 fusion.62
  276.8 6.3 copy.75
  283.1 5.0 copy.74
  288.1 4.4 convolution_convert_fusion.5
  292.6 9.3 %fusion.67 = f32[8,3,1024,64,3]{2,3,4,1,0:T(8,128)} fusion(bf16[8,1024,3,64,1]{1,3,4,2,0:T(8,128)(2,1)S(1)} %bitcast.200, bf16[8,64,3,3,64]{4,1,3,2,0:T(8,128)(2,1)} %copy-done.6), kind=kOutput, calls=%fused_computation.125 | convolution fusion | flops 603979776 | bytes 22609920 | tf_op jit(solution)/shard_map/sqgre,skge->sgrqk/dot_general | solution.py:209
  304.1 11.7 %reduce-scatter.13.cloned.1.call-done = bf16[8,64,576]{2,1,0:T(8,128)(2,1)} async-done(((bf16[8,256,576]{2,1,0:T(8,128)(2,1)}), bf16[8,64,576]{2,1,0:T(8,128)(2,1)}) %reduce-scatter.13.cloned.1.call-update) | async-done | bytes 589840 | tf_op jit(solution)/shard_map/reduce_scatter | solution.py:186
  315.8 2.2 fusion.37
  321.9 2.9 reshape.243
  324.8 3.6 fusion.26
  328.4 10.1 %bitcast_convert_fusion = bf16[8,3,64,1024]{3,2,1,0:T(8,128)(2,1)} fusion(f32[8,3,1024,64,3]{2,3,4,1,0:T(8,128)} %fusion.67, f32[8,3,3,64]{3,2,1,0:T(4,128)S(1)} %copy-done.39, pred[64,1024]{1,0:T(8,128)(4,1)S(1)} %iota_compare_fusion.1, bf16[8,64,3,3,64]{1,0,4,3,2:T(8,128)(2,1)S(1)} %copy-done.18), kind=kOutput, calls=%fused_computation.31 | convolution fusion | flops 624427008 | bytes 22693888 | tf_op jit(solution)/shard_map/sgrqk,sqgre->skge/dot_general | solution.py:230
  338.5 6.2 copy.83
  344.6 11.8 %fusion.12 = bf16[8,3,3,64,1024]{4,3,2,1,0:T(8,128)(2,1)S(1)} fusion(f32[8,3,1024,64,3]{2,3,4,1,0:T(8,128)} %fusion.67, f32[8,3,3,64]{3,2,1,0:T(4,128)S(1)} %copy.78, f32[8,3,3,64]{3,2,1,0:T(4,128)S(1)} %copy-done.39, pred[64,1024]{1,0:T(8,128)(4,1)S(1)} %iota_compare_fusion.1, bf16[8,1024,3,64,1]{1,3,4,2,0:T(8,128)(2,1)} %bitcast.218, ...), kind=kOutput, calls=%fused_computation.20 | convolution fusion | flops 632291328 | bytes 32149504 | tf_op jit(solution)/shard_map/sqgre,skge->sgrqk/dot_general | solution.py:214
  356.5 4.1 fusion.22
  361.1 6.2 copy.82
  367.2 8.3 %pad_maximum_fusion = bf16[8,1024,384]{2,1,0:T(8,128)(2,1)} fusion(bf16[8,1024,192]{2,1,0:T(8,128)(2,1)} %copy.83, bf16[8,1024,192]{2,1,0:T(8,128)(2,1)} %copy.82), kind=kLoop, calls=%fused_computation.30 | loop fusion | flops 12582912 | bytes 12582912 | tf_op jit(solution)/shard_map/concatenate | solution.py:236
  376.5 3.4 bitcast_convert_fusion.1
  380.0 6.3 convolution_multiply_fusion
  390.1 70.2 %reduce-scatter.15.cloned.1.call-done = bf16[8,64,384]{2,1,0:T(8,128)(2,1)} async-done(((bf16[8,1024,384]{2,1,0:T(8,128)(2,1)}), bf16[8,64,384]{2,1,0:T(8,128)(2,1)}) %reduce-scatter.15.cloned.1.call-update) | async-done | bytes 393232 | tf_op jit(solution)/shard_map/reduce_scatter | solution.py:245
  465.7 2.9 convolution_convert_fusion
  468.7 2.6 copy.72
  472.1 24.2 %all-reduce.14.cloned.1.call-done = (bf16[288,384]{1,0:T(8,128)(2,1)}, bf16[288,384]{1,0:T(8,128)(2,1)}, bf16[384,288]{0,1:T(8,128)(2,1)}) async-done(((bf16[288,384]{1,0:T(8,128)(2,1)}, bf16[288,384]{1,0:T(8,128)(2,1)}, bf16[384,288]{0,1:T(8,128)(2,1)}), (bf16[288,384]{1,0:T(8,128)(2,1)}, bf16[288,384]{1,0:T(8,128)(2,1)}, bf16[384,288]{0,1:T(8,128)(2,1)})) %all-reduce.14.cloned.1.call-update) | async-done | bytes 663568 | tf_op jit(solution)/shard_map/psum | solution.py:316
  507.0 8.8 %reduce-scatter.23.cloned.1.call-done = bf16[288,576]{1,0:T(8,128)(2,1)} async-done(((bf16[576,576]{1,0:T(8,128)(2,1)}), bf16[288,576]{1,0:T(8,128)(2,1)}) %reduce-scatter.23.cloned.1.call-update) | async-done | bytes 331792 | tf_op jit(solution)/shard_map/reduce_scatter | solution.py:294
  515.7 19.9 %reduce-scatter.17.cloned.1.call-done = bf16[288,576]{1,0:T(8,128)(2,1)} async-done(((bf16[576,576]{1,0:T(8,128)(2,1)}), bf16[288,576]{1,0:T(8,128)(2,1)}) %reduce-scatter.17.cloned.1.call-update) | async-done | bytes 331792 | tf_op jit(solution)/shard_map/reduce_scatter | solution.py:285
  535.6 14.2 %reduce-scatter.21.cloned.1.call-done = bf16[288,192]{1,0:T(8,128)(2,1)} async-done(((bf16[576,192]{1,0:T(8,128)(2,1)}), bf16[288,192]{1,0:T(8,128)(2,1)}) %reduce-scatter.21.cloned.1.call-update) | async-done | bytes 110608 | tf_op jit(solution)/shard_map/reduce_scatter | solution.py:291
  549.8 15.0 %reduce-scatter.19.cloned.1.call-done = bf16[288,192]{1,0:T(8,128)(2,1)} async-done(((bf16[576,192]{1,0:T(8,128)(2,1)}), bf16[288,192]{1,0:T(8,128)(2,1)}) %reduce-scatter.19.cloned.1.call-update) | async-done | bytes 110608 | tf_op jit(solution)/shard_map/reduce_scatter | solution.py:288
  564.8 4.9 all-reduce.7
  569.9 34.5 %all-reduce.4 = (bf16[288]{0:T(512)(128)(2,1)S(1)}, bf16[288]{0:T(512)(128)(2,1)S(1)}) all-reduce(bf16[288]{0:T(512)(128)(2,1)S(1)} %dynamic-slice.3, bf16[288]{0:T(512)(128)(2,1)S(1)} %dynamic-slice.5), channel_id=1, replica_groups=mesh['dp'=2,'context'=4,'tensor'=4] {'context','tensor'}, use_global_device_ids=true, to_apply=%region_14.15 | all-reduce | flops 576 | bytes 2304 | tf_op jit(solution)/shard_map/psum | solution.py:308
  605.6 14.5 %reduce-scatter.11.cloned.1.call-done = bf16[8,64,576]{2,1,0:T(8,128)(2,1)} async-done(((bf16[8,256,576]{2,1,0:T(8,128)(2,1)}), bf16[8,64,576]{2,1,0:T(8,128)(2,1)}) %reduce-scatter.11.cloned.1.call-update) | async-done | bytes 589840 | tf_op jit(solution)/shard_map/reduce_scatter | solution.py:168
  620.1 3.5 fusion.42
  623.6 93.3 %all-reduce.12.cloned.1.call-done = (bf16[288,576]{1,0:T(8,128)(2,1)}, bf16[288,192]{1,0:T(8,128)(2,1)}, bf16[288,192]{1,0:T(8,128)(2,1)}, bf16[288,576]{1,0:T(8,128)(2,1)}) async-done(((bf16[288,576]{1,0:T(8,128)(2,1)}, bf16[288,192]{1,0:T(8,128)(2,1)}, bf16[288,192]{1,0:T(8,128)(2,1)}, bf16[288,576]{1,0:T(8,128)(2,1)}), (bf16[288,576]{1,0:T(8,128)(2,1)}, bf16[288,192]{1,0:T(8,128)(2,1)}, ...) | async-done | bytes 884752 | tf_op jit(solution)/shard_map/psum | solution.py:310
  (262 shorter events, 98.2 us)
Async XLA Ops:
  7.2 23.8 %copy-start.8 = (bf16[8,64,576]{2,1,0:T(8,128)(2,1)S(1)}, bf16[8,64,576]{2,1,0:T(8,128)(2,1)}, u32[]{:S(2)}) copy-start(bf16[8,64,576]{2,1,0:T(8,128)(2,1)} %param.13) | copy-start | bytes 1769476
  7.2 89.8 %all-gather.4.cloned.1.call-start = ((), (), s32[]{:S(2)}) async-start(), calls=%async_computation.10 | async-start | bytes 6684672 | tf_op jit(solution)/shard_map/all_gather | solution.py:121
  16.9 14.8 %copy-start.34 = (f32[576]{0:T(1024)}, f32[576]{0:T(1024)S(1)}, u32[]{:S(2)}) copy-start(f32[576]{0:T(1024)S(1)} %convert_element_type.199) | copy-start | bytes 6916
  18.2 13.5 %copy-start.36 = (f32[8,64]{1,0:T(8,128)}, f32[8,64]{1,0:T(8,128)S(1)}, u32[]{:S(2)}) copy-start(f32[8,64]{1,0:T(8,128)S(1)} %add_rsqrt_fusion.1) | copy-start | bytes 6148
  31.2 11.1 %copy-start.10 = (bf16[8,64,576]{2,1,0:T(8,128)(2,1)}, bf16[8,64,576]{2,1,0:T(8,128)(2,1)S(1)}, u32[]{:S(2)}) copy-start(bf16[8,64,576]{2,1,0:T(8,128)(2,1)S(1)} %fusion.38) | copy-start | bytes 1769476
  32.2 1.6 copy-start.29
  33.7 163.3 %all-gather.6.cloned.1.call-start = ((), (), s32[]{:S(2)}) async-start(), calls=%async_computation.11 | async-start | bytes 3276800 | tf_op jit(solution)/shard_map/all_gather | solution.py:156
  45.8 2.0 copy-start.30
  138.1 3.2 copy-start.6
  141.3 2.9 copy-start.31
  141.4 11.2 %copy-start.32 = (bf16[288,384]{1,0:T(8,128)(2,1)S(1)}, bf16[288,384]{1,0:T(8,128)(2,1)}, u32[]{:S(2)}) copy-start(bf16[288,384]{1,0:T(8,128)(2,1)} %param.21) | copy-start | bytes 663556
  141.4 18.7 %copy-start.33 = (bf16[384,288]{0,1:T(8,128)(2,1)S(1)}, bf16[384,288]{0,1:T(8,128)(2,1)}, u32[]{:S(2)}) copy-start(bf16[384,288]{0,1:T(8,128)(2,1)} %param.22) | copy-start | bytes 663556
  143.4 108.7 %all-gather.8.cloned.1.call-start = ((), (), s32[]{:S(2)}) async-start(), calls=%async_computation.13 | async-start | bytes 3276800 | tf_op jit(solution)/shard_map/all_gather | solution.py:172
  144.2 171.6 %reduce-scatter.13.cloned.1.call-start = ((), (), s32[]{:S(2)}) async-start(), calls=%async_computation.14 | async-start | bytes 3276800 | tf_op jit(solution)/shard_map/reduce_scatter | solution.py:186
  197.0 3.6 copy-start.1
  197.0 3.6 copy-start.20
  252.2 6.8 copy-start.21
  259.0 1.6 copy-start.15
  259.0 1.6 copy-start.19
  264.6 1.7 copy-start.38
  264.6 111.0 %reduce-scatter.29.cloned.1.call-start = ((), (), s32[]{:S(2)}) async-start(), calls=%async_computation.22 | async-start | bytes 663552 | tf_op jit(solution)/shard_map/reduce_scatter | solution.py:303
  270.0 105.7 %reduce-scatter.25.cloned.1.call-start = ((), (), s32[]{:S(2)}) async-start(), calls=%async_computation.20 | async-start | bytes 663552 | tf_op jit(solution)/shard_map/reduce_scatter | solution.py:297
  292.5 83.2 %reduce-scatter.27.cloned.1.call-start = ((), (), s32[]{:S(2)}) async-start(), calls=%async_computation.21 | async-start | bytes 663552 | tf_op jit(solution)/shard_map/reduce_scatter | solution.py:300
  292.5 9.3 %copy-start.2 = (bf16[8,256,576]{2,1,0:T(8,128)(2,1)S(1)}, bf16[8,256,576]{2,1,0:T(8,128)(2,1)}, u32[]{:S(2)}) copy-start(bf16[8,256,576]{2,1,0:T(8,128)(2,1)} %all-gather.6.cloned.1.call-done) | copy-start | bytes 7077892
  292.6 9.3 %copy-start.16 = (bf16[2048,384]{1,0:T(8,128)(2,1)S(1)}, bf16[2048,384]{1,0:T(8,128)(2,1)}, u32[]{:S(2)}) copy-start(bf16[2048,384]{1,0:T(8,128)(2,1)} %copy-done.15) | copy-start | bytes 4718596
  304.0 156.3 %reduce-scatter.15.cloned.1.call-start = ((), (), s32[]{:S(2)}) async-start(), calls=%async_computation.15 | async-start | bytes 6684672 | tf_op jit(solution)/shard_map/reduce_scatter | solution.py:245
  315.8 2.2 copy-start.4
  315.8 2.2 copy-start.17
  315.8 4.6 copy-start.22
  321.9 6.5 copy-start.39
  324.8 3.7 copy-start.18
  344.6 11.9 %copy-start.7 = (bf16[8,64,3,3,64]{4,1,3,2,0:T(8,128)(2,1)S(1)}, bf16[8,64,3,3,64]{4,1,3,2,0:T(8,128)(2,1)}, u32[]{:S(2)}) copy-start(bf16[8,64,3,3,64]{4,1,3,2,0:T(8,128)(2,1)} %copy-done.6) | copy-start | bytes 1769476
  356.5 4.5 copy-start
  375.6 120.7 %all-reduce.14.cloned.1.call-start = ((), (), s32[]{:S(2)}) async-start(), calls=%async_computation.24 | async-start | bytes 1327104 | tf_op jit(solution)/shard_map/psum | solution.py:316
  376.3 139.4 %reduce-scatter.23.cloned.1.call-start = ((), (), s32[]{:S(2)}) async-start(), calls=%async_computation.19 | async-start | bytes 1105920 | tf_op jit(solution)/shard_map/reduce_scatter | solution.py:294
  379.9 155.7 %reduce-scatter.17.cloned.1.call-start = ((), (), s32[]{:S(2)}) async-start(), calls=%async_computation.16 | async-start | bytes 1105920 | tf_op jit(solution)/shard_map/reduce_scatter | solution.py:285
  390.1 159.7 %reduce-scatter.21.cloned.1.call-start = ((), (), s32[]{:S(2)}) async-start(), calls=%async_computation.18 | async-start | bytes 442368 | tf_op jit(solution)/shard_map/reduce_scatter | solution.py:291
  460.3 2.2 copy-start.27
  463.8 101.0 %reduce-scatter.19.cloned.1.call-start = ((), (), s32[]{:S(2)}) async-start(), calls=%async_computation.17 | async-start | bytes 442368 | tf_op jit(solution)/shard_map/reduce_scatter | solution.py:288
  465.7 154.4 %reduce-scatter.11.cloned.1.call-start = ((), (), s32[]{:S(2)}) async-start(), calls=%async_computation.12 | async-start | bytes 3276800 | tf_op jit(solution)/shard_map/reduce_scatter | solution.py:168
  471.2 30.2 %copy-start.14 = (bf16[576,576]{1,0:T(8,128)(2,1)S(1)}, bf16[576,576]{1,0:T(8,128)(2,1)}, u32[]{:S(2)}) copy-start(bf16[576,576]{1,0:T(8,128)(2,1)} %copy-done.13) | copy-start | bytes 1990660
  471.3 30.8 %copy-start.24 = (bf16[576,192]{1,0:T(8,128)(2,1)S(1)}, bf16[576,192]{1,0:T(8,128)(2,1)}, u32[]{:S(2)}) copy-start(bf16[576,192]{1,0:T(8,128)(2,1)} %copy-done.23) | copy-start | bytes 663556
  471.3 245.6 %all-reduce.12.cloned.1.call-start = ((), (), s32[]{:S(2)}) async-start(), calls=%async_computation.23 | async-start | bytes 2064384 | tf_op jit(solution)/shard_map/psum | solution.py:310
  499.7 3.7 copy-start.26
  503.4 3.1 copy-start.9
  503.4 3.1 copy-start.35
  503.4 3.1 copy-start.37
  506.4 113.6 %copy-start.5 = (f32[8,64,576]{2,1,0:T(8,128)S(1)}, f32[8,64,576]{2,1,0:T(8,128)}, u32[]{:S(2)}) copy-start(f32[8,64,576]{2,1,0:T(8,128)} %copy-done.3) | copy-start | bytes 3538948
  (7 other events, 7.8 us)
Sparse Core Ops, SparseCore 0:
  33.8 63.1 all-gather.3
  143.6 53.4 all-gather.5
  198.6 53.5 all-gather.7
  264.8 51.0 reduce-scatter.12
  318.5 13.2 reduce-scatter.28
  334.5 13.6 reduce-scatter.24
  351.1 13.7 reduce-scatter.26
  375.7 84.6 reduce-scatter.14
  462.9 33.2 all-reduce.13
  498.3 17.3 reduce-scatter.22
  518.6 16.9 reduce-scatter.16
  537.7 12.0 reduce-scatter.20
  552.6 12.1 reduce-scatter.18
  566.9 53.1 reduce-scatter.10
  623.8 93.1 all-reduce.11
where the time goes:
time: 739 us; the launch traced here: 731 us
  waiting for transfers between devices  392 us (53%)
  matrix products  99.6 us (13%)
  blocking collectives  96.6 us (13%)
  local copies, waits for them, and re-layouts  71.4 us (10%)
  other arithmetic  53.2 us (7%)
  between operations  16.3 us (2%)
    psum x1, waiting for transfers between devices, body(): lax.psum(shards[2].astype(jnp.bfloat16), ('context', 'tensor'))  93.3 us
    reduce_scatter x1, waiting for transfers between devices, body(): lax.psum_scatter(grad_kv.astype(jnp.bfloat16), ('context', 'tensor'), sca...  70.2 us
    all_gather x1, waiting for transfers between devices, body(): lax.all_gather(out_grad, 'tensor', axis=1, tiled=True)  48.1 us
    all_gather x1, waiting for transfers between devices, body(): lax.all_gather(kv_local, ('context', 'tensor'), axis=1, tiled=True)  40.9 us
    psum x1, blocking collectives, body(): lax.psum(shards[0].astype(jnp.bfloat16), ('context', 'tensor'))  34.5 us
    all_gather x1, waiting for transfers between devices, body(): ffn_rows = lax.all_gather(ffn_low, 'tensor', axis=1, tiled=True)  30.1 us
    psum x1, waiting for transfers between devices, body(): lax.psum(shards[6].astype(jnp.bfloat16), 'context').astype(jnp.float32)  24.2 us
    reduce_scatter x1, waiting for transfers between devices, body(): lax.psum_scatter(query_grad.astype(jnp.bfloat16), 'dp', scatter_dimension...  19.9 us
  transfers between devices with their start and end apart: 15, of which 12 were waited for; matrix products, arithmetic and copies ran while one was open for 20% of the time, Pallas kernels for 0%

commit v1 on v0

--- a/solution.py
+++ b/solution.py
@@ -118,7 +118,29 @@
         .reshape(seq_count, local_len, kv_width)
     )
     kv_local = jnp.concatenate([keys_low, value_rows.astype(jnp.bfloat16)], axis=-1)
-    kv_whole = lax.all_gather(kv_local, ("context", "tensor"), axis=1, tiled=True)
+    ways, here, step = (
+        lax.axis_size(("context", "tensor")),
+        lax.axis_index(("context", "tensor")),
+        kv_local.shape[1],
+    )
+    shape = [n * ways if d == 1 else n for d, n in enumerate(kv_local.shape)]
+    full = lax.dynamic_update_slice_in_dim(
+        jnp.zeros(shape, kv_local.dtype), kv_local, here * step, axis=1
+    )
+    going_up = going_down = kv_local
+    for far in range(1, ways // 2 + 1):
+        going_up = lax.ppermute(
+            going_up, ("context", "tensor"), [(d, (d + 1) % ways) for d in range(ways)]
+        )
+        full = lax.dynamic_update_slice_in_dim(full, going_up, (here - far) % ways * step, axis=1)
+        if 2 * far < ways:
+            going_down = lax.ppermute(
+                going_down, ("context", "tensor"), [(d, (d - 1) % ways) for d in range(ways)]
+            )
+            full = lax.dynamic_update_slice_in_dim(
+                full, going_down, (here + far) % ways * step, axis=1
+            )
+    kv_whole = full
     seq_len = kv_whole.shape[1]
     query_groups = queries_low.reshape(seq_count, local_len, KV_HEADS, repeat, HEAD_DIM)
 

time: 739 us -> 999 us (1.35)
  local copies, waits for them, and re-layouts: 71.4 us -> 202 us
  starting transfers between devices: 1 us -> 72.7 us
  waiting for transfers between devices: 392 us -> 441 us
    dynamic_update_slice x0 -> x16, local copies, waits for them, and re-layouts: none -> 107 us  [the longest x8 52.7 us: body(): lax.dynamic_update_slice_in_dim(full, going_up, (here - far) % ways * ste...]
    ppermute x0 -> x15, starting transfers between devices: none -> 71.9 us  [the longest x8 55.9 us: body(): lax.ppermute(going_up, ('context', 'tensor'), [(d, (d + 1) % ways) for d...]
    ppermute x0 -> x15, waiting for transfers between devices: none -> 40.3 us  [the longest x8 39.4 us: body(): lax.ppermute(going_up, ('context', 'tensor'), [(d, (d + 1) % ways) for d...]
    reduce_scatter x1, waiting for transfers between devices: 11.7 us -> 46.5 us  [body(): lax.psum_scatter(grad_ffn_part.astype(jnp.bfloat16), 'tensor', scatter_di...]
    psum x1, waiting for transfers between devices: 93.3 us -> 70.6 us  [body(): lax.psum(shards[2].astype(jnp.bfloat16), ('context', 'tensor'))]
    ppermute x0 -> x15, local copies, waits for them, and re-layouts: none -> 20.8 us  [the longest x8 11.2 us: body(): lax.ppermute(going_up, ('context', 'tensor'), [(d, (d + 1) % ways) for d...]
    dynamic_slice x16 -> x0, local copies, waits for them, and re-layouts: 12.1 us -> none  [body(): attended, log_sums = lax.map(attend_one, (query_groups, kv_whole))]
    all_gather x1, waiting for transfers between devices: 40.9 us -> 29.9 us  [body(): piece = lax.all_gather(kv_local, ('context', 'tensor'), axis=1, tiled=True)]
  transfers between devices with their start and end apart: 15 -> 30, of which waited for: 12 -> 20; matrix products, arithmetic and copies ran while one was open for 20% -> 28% of each run, Pallas kernels for 0% -> 0%
where the time goes in v1:
time: 999 us; the launch traced here: 988 us
  waiting for transfers between devices  441 us (44%)
  local copies, waits for them, and re-layouts  202 us (20%)
  matrix products  105 us (11%)
  blocking collectives  97.3 us (10%)
  starting transfers between devices  72.7 us (7%)
  other arithmetic  51.5 us (5%)
  between operations  18.2 us (2%)
    psum x1, waiting for transfers between devices, body(): lax.psum(shards[2].astype(jnp.bfloat16), ('context', 'tensor'))  70.6 us
    reduce_scatter x1, waiting for transfers between devices, body(): lax.psum_scatter(grad_kv.astype(jnp.bfloat16), ('context', 'tensor'), sca...  69.3 us
    ppermute x8, starting transfers between devices, body(): lax.ppermute(going_up, ('context', 'tensor'), [(d, (d + 1) % ways) for d...  55.9 us
    dynamic_update_slice x8, local copies, waits for them, and re-layouts, body(): lax.dynamic_update_slice_in_dim(full, going_up, (here - far) % ways * ste...  52.7 us
    dynamic_update_slice x7, local copies, waits for them, and re-layouts, body(): lax.dynamic_update_slice_in_dim(full, going_down, (here + far) % ways * s...  48.3 us
    all_gather x1, waiting for transfers between devices, body(): lax.all_gather(out_grad, 'tensor', axis=1, tiled=True)  46.6 us
    reduce_scatter x1, waiting for transfers between devices, body(): lax.psum_scatter(grad_ffn_part.astype(jnp.bfloat16), 'tensor', scatter_di...  46.5 us
    ppermute x8, waiting for transfers between devices, body(): lax.ppermute(going_up, ('context', 'tensor'), [(d, (d + 1) % ways) for d...  39.4 us
  transfers between devices with their start and end apart: 30, of which 20 were waited for; matrix products, arithmetic and copies ran while one was open for 28% of the time, Pallas kernels for 0%

profile of v1, /device:TPU:0, one launch (start us, length us, event | category | flops | bytes accessed | tf_op | source)
XLA Modules:
  0.0 987.8 jit_solution(1084754415344416647)
XLA Ops:
  38.2 8.9 collective-permute-done
  47.1 6.4 collective-permute-start.2
  56.3 7.8 collective-permute-done.2
  64.0 9.6 collective-permute-start.4
  74.7 6.4 collective-permute-done.4
  81.1 10.1 %collective-permute-start.6 = (bf16[8,64,384]{2,1,0:T(8,128)(2,1)S(1)}, bf16[8,64,384]{2,1,0:T(8,128)(2,1)S(1)}, u32[]{:S(2)}, u32[]{:S(2)}) collective-permute-start(bf16[8,64,384]{2,1,0:T(8,128)(2,1)S(1)} %collective-permute-done.4), channel_id=1, source_target_pairs={{0,1},{1,2},{2,3},{3,4},{4,5},{5,6},{6,7},{7,8},{8,9},{9,10},{10,1... | collective-permute-start | bytes 1179656 | tf_op jit(solution)/shard_map/ppermute | solution.py:132
  93.8 6.6 collective-permute-done.6
  100.5 7.5 collective-permute-start.8
  116.2 9.8 collective-permute-start.10
  129.3 6.3 collective-permute-done.10
  135.5 7.8 collective-permute-start.12
  143.3 9.0 all_gather.39
  173.4 10.9 %all_gather.40 = bf16[576,576]{1,0:T(8,128)(2,1)S(1)} all-gather(bf16[288,576]{1,0:T(8,128)(2,1)S(1)} %copy-done.41), channel_id=1, replica_groups=mesh['dp'=2,'context'=4,'tensor'=4] {'dp'}, dimensions={0}, use_global_device_ids=true | all-gather | bytes 995328 | tf_op jit(solution)/shard_map/all_gather | solution.py:88
  185.9 6.9 dynamic_update_slice.57
  194.2 7.5 dynamic_update_slice.58
  217.3 7.4 dynamic_update_slice.61
  226.0 7.4 dynamic_update_slice.62
  249.7 7.4 dynamic_update_slice.65
  258.5 7.4 dynamic_update_slice.66
  282.1 7.4 dynamic_update_slice.69
  290.9 7.8 dynamic_update_slice.70
  306.2 38.5 %while.13 = (s32[]{:T(128)}, f32[8,64,576]{1,2,0:T(8,128)}, f32[8,3,3,64]{3,2,1,0:T(4,128)}, bf16[8,1024,384]{1,2,0:T(8,128)(2,1)}, bf16[8,64,3,3,64]{4,1,3,2,0:T(8,128)(2,1)S(1)}, /*index=5*/s32[]{:T(128)}, s32[]{:T(128)}) while((s32[]{:T(128)}, f32[8,64,576]{1,2,0:T(8,128)}, f32[8,3,3,64]{3,2,1,0:T(4,128)}, ...), condition=%wide.region_4.5_spmd.clone, body=%wide.region_1.4_spmd.clone.sunk | while | flops 158137856 | bytes 12032361 | solution.py:169
  350.6 7.0 all_gather.43
  357.6 6.6 all_gather.44
  364.2 6.7 all_gather.45
  370.9 36.8 %all-gather.4.cloned.1.call-done = bf16[8,256,576]{2,1,0:T(8,128)(2,1)} async-done(((bf16[8,64,576]{2,1,0:T(8,128)(2,1)}), bf16[8,256,576]{2,1,0:T(8,128)(2,1)}) %all-gather.4.cloned.1.call-update) | async-done | bytes 2359312 | tf_op jit(solution)/shard_map/all_gather | solution.py:178
  416.2 46.6 %all-gather.6.cloned.1.call-done = bf16[8,256,576]{2,1,0:T(8,128)(2,1)} async-done(((bf16[8,64,576]{2,1,0:T(8,128)(2,1)}), bf16[8,256,576]{2,1,0:T(8,128)(2,1)}) %all-gather.6.cloned.1.call-update) | async-done | bytes 2359312 | tf_op jit(solution)/shard_map/all_gather | solution.py:194
  462.8 7.7 multiply_convert_fusion
  492.9 46.5 %reduce-scatter.13.cloned.1.call-done = bf16[8,64,576]{2,1,0:T(8,128)(2,1)} async-done(((bf16[8,256,576]{2,1,0:T(8,128)(2,1)}), bf16[8,64,576]{2,1,0:T(8,128)(2,1)}) %reduce-scatter.13.cloned.1.call-update) | async-done | bytes 589840 | tf_op jit(solution)/shard_map/reduce_scatter | solution.py:208
  549.2 29.9 %all-gather.8.cloned.1.call-done = bf16[8,1024,384]{2,1,0:T(8,128)(2,1)} async-done(((bf16[8,64,384]{2,1,0:T(8,128)(2,1)}), bf16[8,1024,384]{2,1,0:T(8,128)(2,1)}) %all-gather.8.cloned.1.call-update) | async-done | bytes 6291472 | tf_op jit(solution)/shard_map/all_gather | solution.py:226
  579.0 6.7 fusion.62
  585.7 6.3 copy.120
  597.0 9.2 fusion.67
  606.2 10.0 %bitcast_convert_fusion = bf16[8,3,64,1024]{3,2,1,0:T(8,128)(2,1)} fusion(f32[8,3,1024,64,3]{2,3,4,1,0:T(8,128)} %fusion.67, f32[8,3,3,64]{3,2,1,0:T(4,128)S(1)} %copy-done.58, pred[64,1024]{1,0:T(8,128)(4,1)S(1)} %copy-done.53, bf16[8,64,3,3,64]{1,0,4,3,2:T(8,128)(2,1)S(1)} %copy-done.19), kind=kOutput, calls=%fused_computation.31 | convolution fusion | flops 624427008 | bytes 22693888 | tf_op jit(solution)/shard_map/sgrqk,sqgre->skge/dot_general | solution.py:252
  616.2 6.2 copy.128
  622.4 12.0 %fusion.12 = bf16[8,3,3,64,1024]{4,3,2,1,0:T(8,128)(2,1)S(1)} fusion(f32[8,3,1024,64,3]{2,3,4,1,0:T(8,128)} %fusion.67, f32[8,3,3,64]{3,2,1,0:T(4,128)S(1)} %copy-done.54, f32[8,3,3,64]{3,2,1,0:T(4,128)S(1)} %copy-done.58, pred[64,1024]{1,0:T(8,128)(4,1)S(1)} %copy-done.53, bf16[8,1024,3,64,1]{1,3,4,2,0:T(8,128)(2,1)} %bitcast.218, ...), kind=kOutput, calls=%fused_computation.20 | convolution fusion | flops 632291328 | bytes 32149504 | tf_op jit(solution)/shard_map/sqgre,skge->sgrqk/dot_general | solution.py:236
  638.9 6.1 copy.127
  645.1 8.3 pad_maximum_fusion
  657.6 6.3 convolution_multiply_fusion
  667.9 69.3 %reduce-scatter.15.cloned.1.call-done = bf16[8,64,384]{2,1,0:T(8,128)(2,1)} async-done(((bf16[8,1024,384]{2,1,0:T(8,128)(2,1)}), bf16[8,64,384]{2,1,0:T(8,128)(2,1)}) %reduce-scatter.15.cloned.1.call-update) | async-done | bytes 393232 | tf_op jit(solution)/shard_map/reduce_scatter | solution.py:267
  749.2 23.8 %all-reduce.14.cloned.1.call-done = (bf16[288,384]{1,0:T(8,128)(2,1)}, bf16[288,384]{1,0:T(8,128)(2,1)}, bf16[384,288]{0,1:T(8,128)(2,1)}) async-done(((bf16[288,384]{1,0:T(8,128)(2,1)}, bf16[288,384]{1,0:T(8,128)(2,1)}, bf16[384,288]{0,1:T(8,128)(2,1)}), (bf16[288,384]{1,0:T(8,128)(2,1)}, bf16[288,384]{1,0:T(8,128)(2,1)}, bf16[384,288]{0,1:T(8,128)(2,1)})) %all-reduce.14.cloned.1.call-update) | async-done | bytes 663568 | tf_op jit(solution)/shard_map/psum | solution.py:338
  783.8 8.9 reduce-scatter.23.cloned.1.call-done
  792.7 19.7 %reduce-scatter.17.cloned.1.call-done = bf16[288,576]{1,0:T(8,128)(2,1)} async-done(((bf16[576,576]{1,0:T(8,128)(2,1)}), bf16[288,576]{1,0:T(8,128)(2,1)}) %reduce-scatter.17.cloned.1.call-update) | async-done | bytes 331792 | tf_op jit(solution)/shard_map/reduce_scatter | solution.py:307
  812.4 14.4 %reduce-scatter.21.cloned.1.call-done = bf16[288,192]{1,0:T(8,128)(2,1)} async-done(((bf16[576,192]{1,0:T(8,128)(2,1)}), bf16[288,192]{1,0:T(8,128)(2,1)}) %reduce-scatter.21.cloned.1.call-update) | async-done | bytes 110608 | tf_op jit(solution)/shard_map/reduce_scatter | solution.py:313
  826.8 14.8 %reduce-scatter.19.cloned.1.call-done = bf16[288,192]{1,0:T(8,128)(2,1)} async-done(((bf16[576,192]{1,0:T(8,128)(2,1)}), bf16[288,192]{1,0:T(8,128)(2,1)}) %reduce-scatter.19.cloned.1.call-update) | async-done | bytes 110608 | tf_op jit(solution)/shard_map/reduce_scatter | solution.py:310
  846.7 34.2 %all-reduce.4 = (bf16[288]{0:T(512)(128)(2,1)S(1)}, bf16[288]{0:T(512)(128)(2,1)S(1)}) all-reduce(bf16[288]{0:T(512)(128)(2,1)S(1)} %dynamic-slice.3, bf16[288]{0:T(512)(128)(2,1)S(1)} %dynamic-slice.5), channel_id=1, replica_groups=mesh['dp'=2,'context'=4,'tensor'=4] {'context','tensor'}, use_global_device_ids=true, to_apply=%region_14.15 | all-reduce | flops 576 | bytes 2304 | tf_op jit(solution)/shard_map/psum | solution.py:330
  882.1 16.9 %reduce-scatter.11.cloned.1.call-done = bf16[8,64,576]{2,1,0:T(8,128)(2,1)} async-done(((bf16[8,256,576]{2,1,0:T(8,128)(2,1)}), bf16[8,64,576]{2,1,0:T(8,128)(2,1)}) %reduce-scatter.11.cloned.1.call-update) | async-done | bytes 589840 | tf_op jit(solution)/shard_map/reduce_scatter | solution.py:190
  902.6 70.6 %all-reduce.12.cloned.1.call-done = (bf16[288,576]{1,0:T(8,128)(2,1)}, bf16[288,192]{1,0:T(8,128)(2,1)}, bf16[288,192]{1,0:T(8,128)(2,1)}, bf16[288,576]{1,0:T(8,128)(2,1)}) async-done(((bf16[288,576]{1,0:T(8,128)(2,1)}, bf16[288,192]{1,0:T(8,128)(2,1)}, bf16[288,192]{1,0:T(8,128)(2,1)}, bf16[288,576]{1,0:T(8,128)(2,1)}), (bf16[288,576]{1,0:T(8,128)(2,1)}, bf16[288,192]{1,0:T(8,128)(2,1)}, ...) | async-done | bytes 884752 | tf_op jit(solution)/shard_map/psum | solution.py:332
  (355 shorter events, 271.5 us)
Async XLA Ops:
  8.0 399.7 %all-gather.4.cloned.1.call-start = ((), (), s32[]{:S(2)}) async-start(), calls=%async_computation.10 | async-start | bytes 3276800 | tf_op jit(solution)/shard_map/all_gather | solution.py:178
  32.1 120.7 %copy-start.9 = (bf16[8,64,576]{2,1,0:T(8,128)(2,1)}, bf16[8,64,576]{2,1,0:T(8,128)(2,1)S(1)}, u32[]{:S(2)}) copy-start(bf16[8,64,576]{2,1,0:T(8,128)(2,1)S(1)} %fusion.38) | copy-start | bytes 1769476
  33.1 123.5 %copy-start.30 = (f32[64,32]{0,1:T(8,128)}, f32[64,32]{0,1:T(8,128)S(1)}, u32[]{:S(2)}) copy-start(f32[64,32]{0,1:T(8,128)S(1)} %get-tuple-element.112) | copy-start | bytes 24580
  33.7 124.0 %copy-start.20 = (bf16[8,64,384]{2,1,0:T(8,128)(2,1)}, bf16[8,64,384]{2,1,0:T(8,128)(2,1)S(1)}, u32[]{:S(2)}) copy-start(bf16[8,64,384]{2,1,0:T(8,128)(2,1)S(1)} %pad_maximum_fusion.3) | copy-start | bytes 1179652
  33.7 13.4 %collective-permute-start = (bf16[8,64,384]{2,1,0:T(8,128)(2,1)S(1)}, bf16[8,64,384]{2,1,0:T(8,128)(2,1)S(1)}, u32[]{:S(2)}, u32[]{:S(2)}) collective-permute-start(bf16[8,64,384]{2,1,0:T(8,128)(2,1)S(1)} %pad_maximum_fusion.3), channel_id=1, source_target_pairs={{0,1},{1,2},{2,3},{3,4},{4,5},{5,6},{6,7},{7,8},{8,9},{9,10},{10,1... | collective-permute-start | bytes 1179656 | tf_op jit(solution)/shard_map/ppermute | solution.py:132
  35.8 18.4 %collective-permute-start.1 = (bf16[8,64,384]{2,1,0:T(8,128)(2,1)S(1)}, bf16[8,64,384]{2,1,0:T(8,128)(2,1)S(1)}, u32[]{:S(2)}, u32[]{:S(2)}) collective-permute-start(bf16[8,64,384]{2,1,0:T(8,128)(2,1)S(1)} %pad_maximum_fusion.3), channel_id=1, source_target_pairs={{0,15},{1,0},{2,1},{3,2},{4,3},{5,4},{6,5},{7,6},{8,7},{9,8},{10,9... | collective-permute-start | bytes 1179656 | tf_op jit(solution)/shard_map/ppermute | solution.py:137
  47.1 105.2 %copy-start.34 = (bf16[8,64,384]{2,1,0:T(8,128)(2,1)}, bf16[8,64,384]{2,1,0:T(8,128)(2,1)S(1)}, u32[]{:S(2)}) copy-start(bf16[8,64,384]{2,1,0:T(8,128)(2,1)S(1)} %collective-permute-done) | copy-start | bytes 1179652
  47.1 16.9 %collective-permute-start.2 = (bf16[8,64,384]{2,1,0:T(8,128)(2,1)S(1)}, bf16[8,64,384]{2,1,0:T(8,128)(2,1)S(1)}, u32[]{:S(2)}, u32[]{:S(2)}) collective-permute-start(bf16[8,64,384]{2,1,0:T(8,128)(2,1)S(1)} %collective-permute-done), channel_id=1, source_target_pairs={{0,1},{1,2},{2,3},{3,4},{4,5},{5,6},{6,7},{7,8},{8,9},{9,10},{10,1... | collective-permute-start | bytes 1179656 | tf_op jit(solution)/shard_map/ppermute | solution.py:132
  54.2 81.3 %copy-start.32 = (bf16[8,64,384]{2,1,0:T(8,128)(2,1)}, bf16[8,64,384]{2,1,0:T(8,128)(2,1)S(1)}, u32[]{:S(2)}) copy-start(bf16[8,64,384]{2,1,0:T(8,128)(2,1)S(1)} %collective-permute-done.1) | copy-start | bytes 1179652
  54.2 19.4 %collective-permute-start.3 = (bf16[8,64,384]{2,1,0:T(8,128)(2,1)S(1)}, bf16[8,64,384]{2,1,0:T(8,128)(2,1)S(1)}, u32[]{:S(2)}, u32[]{:S(2)}) collective-permute-start(bf16[8,64,384]{2,1,0:T(8,128)(2,1)S(1)} %collective-permute-done.1), channel_id=1, source_target_pairs={{0,15},{1,0},{2,1},{3,2},{4,3},{5,4},{6,5},{7,6},{8,7},{9,8},{10,9... | collective-permute-start | bytes 1179656 | tf_op jit(solution)/shard_map/ppermute | solution.py:137
  64.0 71.5 %copy-start.33 = (bf16[8,64,384]{2,1,0:T(8,128)(2,1)}, bf16[8,64,384]{2,1,0:T(8,128)(2,1)S(1)}, u32[]{:S(2)}) copy-start(bf16[8,64,384]{2,1,0:T(8,128)(2,1)S(1)} %collective-permute-done.2) | copy-start | bytes 1179652
  64.0 17.1 %collective-permute-start.4 = (bf16[8,64,384]{2,1,0:T(8,128)(2,1)S(1)}, bf16[8,64,384]{2,1,0:T(8,128)(2,1)S(1)}, u32[]{:S(2)}, u32[]{:S(2)}) collective-permute-start(bf16[8,64,384]{2,1,0:T(8,128)(2,1)S(1)} %collective-permute-done.2), channel_id=1, source_target_pairs={{0,1},{1,2},{2,3},{3,4},{4,5},{5,6},{6,7},{7,8},{8,9},{9,10},{10,1... | collective-permute-start | bytes 1179656 | tf_op jit(solution)/shard_map/ppermute | solution.py:132
  73.6 78.7 %copy-start.35 = (bf16[8,64,384]{2,1,0:T(8,128)(2,1)}, bf16[8,64,384]{2,1,0:T(8,128)(2,1)S(1)}, u32[]{:S(2)}) copy-start(bf16[8,64,384]{2,1,0:T(8,128)(2,1)S(1)} %collective-permute-done.3) | copy-start | bytes 1179652
  73.6 17.6 %collective-permute-start.5 = (bf16[8,64,384]{2,1,0:T(8,128)(2,1)S(1)}, bf16[8,64,384]{2,1,0:T(8,128)(2,1)S(1)}, u32[]{:S(2)}, u32[]{:S(2)}) collective-permute-start(bf16[8,64,384]{2,1,0:T(8,128)(2,1)S(1)} %collective-permute-done.3), channel_id=1, source_target_pairs={{0,15},{1,0},{2,1},{3,2},{4,3},{5,4},{6,5},{7,6},{8,7},{9,8},{10,9... | collective-permute-start | bytes 1179656 | tf_op jit(solution)/shard_map/ppermute | solution.py:137
  81.1 71.3 %copy-start.36 = (bf16[8,64,384]{2,1,0:T(8,128)(2,1)}, bf16[8,64,384]{2,1,0:T(8,128)(2,1)S(1)}, u32[]{:S(2)}) copy-start(bf16[8,64,384]{2,1,0:T(8,128)(2,1)S(1)} %collective-permute-done.4) | copy-start | bytes 1179652
  81.1 19.4 %collective-permute-start.6 = (bf16[8,64,384]{2,1,0:T(8,128)(2,1)S(1)}, bf16[8,64,384]{2,1,0:T(8,128)(2,1)S(1)}, u32[]{:S(2)}, u32[]{:S(2)}) collective-permute-start(bf16[8,64,384]{2,1,0:T(8,128)(2,1)S(1)} %collective-permute-done.4), channel_id=1, source_target_pairs={{0,1},{1,2},{2,3},{3,4},{4,5},{5,6},{6,7},{7,8},{8,9},{9,10},{10,1... | collective-permute-start | bytes 1179656 | tf_op jit(solution)/shard_map/ppermute | solution.py:132
  91.2 61.2 %copy-start.37 = (bf16[8,64,384]{2,1,0:T(8,128)(2,1)}, bf16[8,64,384]{2,1,0:T(8,128)(2,1)S(1)}, u32[]{:S(2)}) copy-start(bf16[8,64,384]{2,1,0:T(8,128)(2,1)S(1)} %collective-permute-done.5) | copy-start | bytes 1179652
  91.2 17.0 %collective-permute-start.7 = (bf16[8,64,384]{2,1,0:T(8,128)(2,1)S(1)}, bf16[8,64,384]{2,1,0:T(8,128)(2,1)S(1)}, u32[]{:S(2)}, u32[]{:S(2)}) collective-permute-start(bf16[8,64,384]{2,1,0:T(8,128)(2,1)S(1)} %collective-permute-done.5), channel_id=1, source_target_pairs={{0,15},{1,0},{2,1},{3,2},{4,3},{5,4},{6,5},{7,6},{8,7},{9,8},{10,9... | collective-permute-start | bytes 1179656 | tf_op jit(solution)/shard_map/ppermute | solution.py:137
  100.5 15.7 %collective-permute-start.8 = (bf16[8,64,384]{2,1,0:T(8,128)(2,1)S(1)}, bf16[8,64,384]{2,1,0:T(8,128)(2,1)S(1)}, u32[]{:S(2)}, u32[]{:S(2)}) collective-permute-start(bf16[8,64,384]{2,1,0:T(8,128)(2,1)S(1)} %collective-permute-done.6), channel_id=1, source_target_pairs={{0,1},{1,2},{2,3},{3,4},{4,5},{5,6},{6,7},{7,8},{8,9},{9,10},{10,1... | collective-permute-start | bytes 1179656 | tf_op jit(solution)/shard_map/ppermute | solution.py:132
  108.2 17.8 %collective-permute-start.9 = (bf16[8,64,384]{2,1,0:T(8,128)(2,1)S(1)}, bf16[8,64,384]{2,1,0:T(8,128)(2,1)}, u32[]{:S(2)}, u32[]{:S(2)}) collective-permute-start(bf16[8,64,384]{2,1,0:T(8,128)(2,1)S(1)} %collective-permute-done.7), channel_id=1, source_target_pairs={{0,15},{1,0},{2,1},{3,2},{4,3},{5,4},{6,5},{7,6},{8,7},{9,8},{10,9... | collective-permute-start | bytes 1179656 | tf_op jit(solution)/shard_map/ppermute | solution.py:137
  116.2 19.3 %collective-permute-start.10 = (bf16[8,64,384]{2,1,0:T(8,128)(2,1)S(1)}, bf16[8,64,384]{2,1,0:T(8,128)(2,1)}, u32[]{:S(2)}, u32[]{:S(2)}) collective-permute-start(bf16[8,64,384]{2,1,0:T(8,128)(2,1)S(1)} %collective-permute-done.8), channel_id=1, source_target_pairs={{0,1},{1,2},{2,3},{3,4},{4,5},{5,6},{6,7},{7,8},{8,9},{9,10},{10,1... | collective-permute-start | bytes 1179656 | tf_op jit(solution)/shard_map/ppermute | solution.py:132
  126.0 27.8 %collective-permute-start.11 = (bf16[8,64,384]{2,1,0:T(8,128)(2,1)}, bf16[8,64,384]{2,1,0:T(8,128)(2,1)}, u32[]{:S(2)}, u32[]{:S(2)}) collective-permute-start(bf16[8,64,384]{2,1,0:T(8,128)(2,1)} %collective-permute-done.9), channel_id=1, source_target_pairs={{0,15},{1,0},{2,1},{3,2},{4,3},{5,4},{6,5},{7,6},{8,7},{9,8},{10,9... | collective-permute-start | bytes 1179656 | tf_op jit(solution)/shard_map/ppermute | solution.py:137
  135.5 18.4 %collective-permute-start.12 = (bf16[8,64,384]{2,1,0:T(8,128)(2,1)}, bf16[8,64,384]{2,1,0:T(8,128)(2,1)}, u32[]{:S(2)}, u32[]{:S(2)}) collective-permute-start(bf16[8,64,384]{2,1,0:T(8,128)(2,1)} %collective-permute-done.10), channel_id=1, source_target_pairs={{0,1},{1,2},{2,3},{3,4},{4,5},{5,6},{6,7},{7,8},{8,9},{9,10},{10,1... | collective-permute-start | bytes 1179656 | tf_op jit(solution)/shard_map/ppermute | solution.py:132
  153.9 135.7 %collective-permute-start.13 = (bf16[8,64,384]{2,1,0:T(8,128)(2,1)}, bf16[8,64,384]{2,1,0:T(8,128)(2,1)}, u32[]{:S(2)}, u32[]{:S(2)}) collective-permute-start(bf16[8,64,384]{2,1,0:T(8,128)(2,1)} %collective-permute-done.11), channel_id=1, source_target_pairs={{0,15},{1,0},{2,1},{3,2},{4,3},{5,4},{6,5},{7,6},{8,7},{9,8},{10,9... | collective-permute-start | bytes 1179656 | tf_op jit(solution)/shard_map/ppermute | solution.py:137
  154.0 144.8 %collective-permute-start.14 = (bf16[8,64,384]{2,1,0:T(8,128)(2,1)}, bf16[8,64,384]{2,1,0:T(8,128)(2,1)}, u32[]{:S(2)}, u32[]{:S(2)}) collective-permute-start(bf16[8,64,384]{2,1,0:T(8,128)(2,1)} %collective-permute-done.12), channel_id=1, source_target_pairs={{0,1},{1,2},{2,3},{3,4},{4,5},{5,6},{6,7},{7,8},{8,9},{9,10},{10,1... | collective-permute-start | bytes 1179656 | tf_op jit(solution)/shard_map/ppermute | solution.py:132
  158.9 383.3 %copy-start.45 = (f32[576]{0:T(1024)}, f32[576]{0:T(1024)S(1)}, u32[]{:S(2)}) copy-start(f32[576]{0:T(1024)S(1)} %convert_element_type.206) | copy-start | bytes 6916
  184.3 160.4 %copy-start.22 = (bf16[576,576]{1,0:T(8,128)(2,1)}, bf16[576,576]{1,0:T(8,128)(2,1)S(1)}, u32[]{:S(2)}) copy-start(bf16[576,576]{1,0:T(8,128)(2,1)S(1)} %all_gather.40) | copy-start | bytes 1990660
  347.8 194.5 %copy-start.47 = (f32[8,64]{1,0:T(8,128)}, f32[8,64]{1,0:T(8,128)S(1)}, u32[]{:S(2)}) copy-start(f32[8,64]{1,0:T(8,128)S(1)} %add_rsqrt_fusion) | copy-start | bytes 6148
  349.8 113.0 %all-gather.6.cloned.1.call-start = ((), (), s32[]{:S(2)}) async-start(), calls=%async_computation.12 | async-start | bytes 3276800 | tf_op jit(solution)/shard_map/all_gather | solution.py:194
  350.6 188.9 %reduce-scatter.13.cloned.1.call-start = ((), (), s32[]{:S(2)}) async-start(), calls=%async_computation.13 | async-start | bytes 3276800 | tf_op jit(solution)/shard_map/reduce_scatter | solution.py:208
  479.4 99.7 %all-gather.8.cloned.1.call-start = ((), (), s32[]{:S(2)}) async-start(), calls=%async_computation.14 | async-start | bytes 6684672 | tf_op jit(solution)/shard_map/all_gather | solution.py:226
  480.0 173.5 %reduce-scatter.29.cloned.1.call-start = ((), (), s32[]{:S(2)}) async-start(), calls=%async_computation.22 | async-start | bytes 663552 | tf_op jit(solution)/shard_map/reduce_scatter | solution.py:325
  484.4 169.0 %reduce-scatter.25.cloned.1.call-start = ((), (), s32[]{:S(2)}) async-start(), calls=%async_computation.20 | async-start | bytes 663552 | tf_op jit(solution)/shard_map/reduce_scatter | solution.py:319
  488.1 165.4 %reduce-scatter.27.cloned.1.call-start = ((), (), s32[]{:S(2)}) async-start(), calls=%async_computation.21 | async-start | bytes 663552 | tf_op jit(solution)/shard_map/reduce_scatter | solution.py:322
  489.1 53.1 %copy-start.17 = (bf16[8,64,576]{2,1,0:T(8,128)(2,1)S(1)}, bf16[8,64,576]{2,1,0:T(8,128)(2,1)}, u32[]{:S(2)}) copy-start(bf16[8,64,576]{2,1,0:T(8,128)(2,1)} %param.23) | copy-start | bytes 1769476
  492.9 244.3 %reduce-scatter.15.cloned.1.call-start = ((), (), s32[]{:S(2)}) async-start(), calls=%async_computation.15 | async-start | bytes 6684672 | tf_op jit(solution)/shard_map/reduce_scatter | solution.py:267
  653.4 119.6 %all-reduce.14.cloned.1.call-start = ((), (), s32[]{:S(2)}) async-start(), calls=%async_computation.24 | async-start | bytes 1327104 | tf_op jit(solution)/shard_map/psum | solution.py:338
  654.1 138.5 %reduce-scatter.23.cloned.1.call-start = ((), (), s32[]{:S(2)}) async-start(), calls=%async_computation.19 | async-start | bytes 1105920 | tf_op jit(solution)/shard_map/reduce_scatter | solution.py:316
  657.6 154.8 %reduce-scatter.17.cloned.1.call-start = ((), (), s32[]{:S(2)}) async-start(), calls=%async_computation.16 | async-start | bytes 1105920 | tf_op jit(solution)/shard_map/reduce_scatter | solution.py:307
  667.8 159.0 %reduce-scatter.21.cloned.1.call-start = ((), (), s32[]{:S(2)}) async-start(), calls=%async_computation.18 | async-start | bytes 442368 | tf_op jit(solution)/shard_map/reduce_scatter | solution.py:313
  740.6 101.0 %reduce-scatter.19.cloned.1.call-start = ((), (), s32[]{:S(2)}) async-start(), calls=%async_computation.17 | async-start | bytes 442368 | tf_op jit(solution)/shard_map/reduce_scatter | solution.py:310
  742.5 156.5 %reduce-scatter.11.cloned.1.call-start = ((), (), s32[]{:S(2)}) async-start(), calls=%async_computation.11 | async-start | bytes 3276800 | tf_op jit(solution)/shard_map/reduce_scatter | solution.py:190
  748.4 224.8 %all-reduce.12.cloned.1.call-start = ((), (), s32[]{:S(2)}) async-start(), calls=%async_computation.23 | async-start | bytes 2064384 | tf_op jit(solution)/shard_map/psum | solution.py:332
  783.3 58.4 %copy-start.57 = (bf16[576]{0:T(1024)(128)(2,1)S(1)}, bf16[576]{0:T(1024)(128)(2,1)}, u32[]{:S(2)}) copy-start(bf16[576]{0:T(1024)(128)(2,1)} %get-tuple-element.61) | copy-start | bytes 3460
  783.3 115.8 %copy-start.4 = (f32[8,64,576]{2,1,0:T(8,128)S(1)}, f32[8,64,576]{2,1,0:T(8,128)}, u32[]{:S(2)}) copy-start(f32[8,64,576]{2,1,0:T(8,128)} %copy-done.2) | copy-start | bytes 3538948
  783.3 115.8 %copy-start.46 = (f32[576]{0:T(1024)S(1)}, f32[576]{0:T(1024)}, u32[]{:S(2)}) copy-start(f32[576]{0:T(1024)} %copy-done.45) | copy-start | bytes 6916
  783.3 115.8 %copy-start.48 = (f32[8,64]{1,0:T(8,128)S(1)}, f32[8,64]{1,0:T(8,128)}, u32[]{:S(2)}) copy-start(f32[8,64]{1,0:T(8,128)} %copy-done.47) | copy-start | bytes 6148
  783.3 115.7 %copy-start.56 = (f32[8,64]{1,0:T(8,128)S(1)}, f32[8,64]{1,0:T(8,128)}, u32[]{:S(2)}) copy-start(f32[8,64]{1,0:T(8,128)} %copy-done.55) | copy-start | bytes 6148
  (41 other events, 470.4 us)
Sparse Core Ops, SparseCore 0:
  349.9 57.7 all-gather.3
  409.2 53.5 all-gather.5
  479.5 59.9 reduce-scatter.12
  542.1 14.1 reduce-scatter.28
  559.0 13.7 reduce-scatter.24
  575.5 13.7 reduce-scatter.26
  653.5 83.6 reduce-scatter.14
  739.7 33.2 all-reduce.13
  775.3 17.3 reduce-scatter.22
  795.4 16.9 reduce-scatter.16
  814.6 12.0 reduce-scatter.20
  829.4 12.1 reduce-scatter.18
  843.9 55.0 reduce-scatter.10
Sparse Core Ops, SparseCore 1:
  482.2 96.8 all-gather.7
  841.7 131.5 all-reduce.11
